TPU v7x, 32 devices: a whole 2x2x4 slice. The times are simulated.
32 devices in a mesh: groups: 2 (over y), seq: 16 (over z, x, core).
Axes of the slice: x: 2, y: 2, z: 4, core: 2. Of those that a mesh axis runs over, the one named last changes fastest.
Arguments:
- xbc: bfloat16 [16384, 2304], P(('groups', 'seq')), parts along dimension 0, may hold values from -24 to 24
- conv_weight: float32 [4, 2304], replicated, may hold values from -3 to 3
- log_decay: float32 [16, 16384], P(None, ('groups', 'seq')), parts along dimension 1, may hold values from -1 to 0, as said below
- level_weights: float32 [16, 14, 16384], P(None, None, ('groups', 'seq')), parts along dimension 2, may hold values from 0.1 to 1
- gain: float32 [2048], replicated, may hold values from 0.25 to 1.75
Outputs:
- mixed: bfloat16 [16384, 2048], P(('groups', 'seq')), parts along dimension 0
There are 2 independent parts, one for each index of `groups`. A program takes and returns all parts, laid end to end along the dimension named above; an argument that names none is the same for every part. Nothing has to cross between parts.
Inputs may be any that keep to these rules, and one draw needn't show every extreme that they name: `log_decay`: every entry is negative.
All inputs are finite; a program needn't handle non-finite values.
Results may differ from a plain program's by a relative error of at most 0.0034.
Values may be sent and summed in bfloat16 or wider, within the bound.
A program may use at most 128 MiB of HBM per device.

v0:
```python
import jax
import jax.numpy as jnp
from jax import lax
from jax.sharding import PartitionSpec as P


def from_behind(block, axis, distance):
    devices = range(lax.axis_size(axis))
    route = [(i - distance, i) for i in devices if i - distance in devices]
    return lax.ppermute(block, axis, route)


def swapped(value, axis, apart):
    return lax.ppermute(value, axis, [(i, i ^ 1 << apart) for i in range(lax.axis_size(axis))])


def bit_length(numbers, limit):
    counted = jnp.zeros(numbers.shape, jnp.int32)
    for power_index in range(limit):
        counted = counted + (numbers >= 1 << power_index).astype(jnp.int32)
    return counted


def compute_near(values_rows, in_map, out_map, local_log, level_gain, head_count):
    row_count = values_rows.shape[0]
    head_dim = values_rows.shape[1] // head_count
    local_bits = row_count.bit_length() - 1
    scores = lax.dot_general(
        out_map, in_map, (((1,), (1,)), ((), ())), preferred_element_type=jnp.float32
    )
    element_index = lax.iota(jnp.int32, row_count)
    level_index = bit_length(
        jnp.bitwise_xor(element_index[:, None], element_index[None, :]), local_bits
    )
    causal = element_index[None, :] <= element_index[:, None]
    chosen = jnp.zeros((head_count, row_count, row_count), jnp.float32)
    for level_step in range(local_bits + 1):
        chosen = jnp.where(
            (level_index == level_step)[None], level_gain[:, level_step, :, None], chosen
        )
    gap_log = jnp.where(causal[None], local_log[:, :, None] - local_log[:, None, :], -1e30)
    weight = (chosen * jnp.exp(gap_log) * scores[None]).astype(jnp.bfloat16)
    shaped = values_rows.reshape(row_count, head_count, head_dim)
    near_heads = jnp.einsum("hts,shp->thp", weight, shaped, preferred_element_type=jnp.float32)
    return near_heads.reshape(row_count, head_count * head_dim)


def silu_conv(xbc, conv_weight):
    kernel = conv_weight.shape[0]
    row_count = xbc.shape[0]
    earlier = from_behind(xbc[row_count - kernel + 1 :], "seq", 1)
    padded = jnp.concatenate([earlier, xbc], axis=0).astype(jnp.float32)
    convolved = padded[0:row_count] * conv_weight[0]
    for offset in range(1, kernel):
        convolved = convolved + padded[offset : offset + row_count] * conv_weight[offset]
    return jax.nn.silu(convolved).astype(jnp.bfloat16)


def combine_groups(aggregate, partner, group_span, partner_span, is_upper, head_dim):
    left_part = jnp.where(is_upper, partner, aggregate)
    right_part = jnp.where(is_upper, aggregate, partner)
    right_span = jnp.where(is_upper, group_span, partner_span)
    carry_decay = jnp.repeat(jnp.exp(right_span), head_dim)
    return left_part * carry_decay[None, :] + right_part


def add_level(running, queries_wide, partner, factor, head_count):
    product = jnp.dot(
        queries_wide, partner, precision=lax.Precision.HIGHEST, preferred_element_type=jnp.float32
    )
    row_count = product.shape[0]
    shaped = product.reshape(row_count, head_count, -1) * factor.T[:, :, None]
    return running + shaped.reshape(row_count, -1)


def on_device(xbc, conv_weight, log_decay, level_weights, gain):
    row_count = xbc.shape[0]
    head_count = log_decay.shape[0]
    inner_width = gain.shape[0]
    head_dim = inner_width // head_count
    state_size = (xbc.shape[1] - inner_width) // 2
    activated = silu_conv(xbc, conv_weight)
    values_rows = activated[:, :inner_width]
    in_map = activated[:, inner_width : inner_width + state_size]
    out_map = activated[:, inner_width + state_size :]
    local_log = jnp.cumsum(log_decay, axis=1)
    block_total = local_log[:, row_count - 1]
    tail_decay = jnp.exp(block_total[:, None] - local_log)
    decayed = (
        (values_rows.reshape(row_count, head_count, head_dim) * tail_decay.T[:, :, None])
        .reshape(row_count, inner_width)
        .astype(jnp.bfloat16)
    )
    block_state = lax.dot_general(
        in_map, decayed, (((0,), (0,)), ((), ())), preferred_element_type=jnp.float32
    )
    local_bits = row_count.bit_length() - 1
    seq_bits = lax.axis_size("seq").bit_length() - 1
    element_index = lax.axis_index("seq")
    queries_wide = out_map.astype(jnp.float32)
    far_term = jnp.zeros((row_count, inner_width), jnp.float32)
    aggregate = block_state
    group_span = block_total
    group_prefix = jnp.zeros_like(block_total)
    for bit_index in range(seq_bits):
        is_upper = element_index >> bit_index & 1 == 1
        partner, partner_span = swapped((aggregate, group_span), "seq", bit_index)
        gap_log = group_prefix
        group_prefix = jnp.where(is_upper, group_prefix + partner_span, group_prefix)
        exponent = jnp.where(is_upper, local_log + gap_log[:, None], -1e30)
        factor = level_weights[:, local_bits + bit_index + 1, :] * jnp.exp(exponent)

        def taken(running):
            return add_level(running, queries_wide, partner, factor, head_count)

        def skipped(running):
            return running

        far_term = lax.cond(is_upper, taken, skipped, far_term)
        if bit_index + 1 < seq_bits:
            aggregate = combine_groups(
                aggregate, partner, group_span, partner_span, is_upper, head_dim
            )
            group_span = group_span + partner_span
    near_term = compute_near(values_rows, in_map, out_map, local_log, level_weights, head_count)
    mixed_sum = (near_term + far_term).reshape(row_count, head_count, head_dim)
    inv_rms = lax.rsqrt(jnp.mean(mixed_sum * mixed_sum, axis=2, keepdims=True) + 1e-05)
    return ((mixed_sum * inv_rms).reshape(row_count, inner_width) * gain).astype(jnp.bfloat16)


def solution(mesh):
    in_specs = (
        P(("groups", "seq"), None),
        P(),
        P(None, ("groups", "seq")),
        P(None, None, ("groups", "seq")),
        P(),
    )
    out_specs = P(("groups", "seq"), None)
    return jax.shard_map(
        on_device, mesh=mesh, in_specs=in_specs, out_specs=out_specs, check_vma=False
    )
```

profile of v0, /device:TPU:31, one launch (start us, length us, event | category | flops | bytes accessed | tf_op | source)
XLA Modules:
  0.0 186.8 jit_solution(15527379835954160170)
XLA Ops:
  5.0 2.1 %maximum_convert_fusion = f32[515,2304]{1,0:T(8,128)S(1)} fusion(bf16[512,2304]{1,0:T(8,128)(2,1)} %param.13, bf16[3,2304]{1,0:T(4,128)(2,1)S(1)} %collective-permute-done), kind=kLoop, calls=%fused_computation.67 | loop fusion | flops 4746240 | bytes 7119360 | tf_op jit(solution)/shard_map/convert_element_type | solution.py:52
  7.2 2.9 %multiply_convert_fusion.2 = bf16[512,2304]{1,0:T(8,128)(2,1)S(1)} fusion(f32[515,2304]{1,0:T(8,128)S(1)} %maximum_convert_fusion, f32[2304]{0:T(1024)S(1)} %get-tuple-element.290, f32[2304]{0:T(1024)S(1)} %get-tuple-element.291, f32[2304]{0:T(1024)S(1)} %get-tuple-element.289, f32[2304]{0:T(1024)S(1)} %get-tuple-element.288), kind=kLoop, calls=%fused_computation.60 | loop fusion | flops 14155776 | bytes 21270528 | tf_op jit(solution)/shard_map/convert_element_type | solution.py:56
  11.2 2.5 %fusion.46 = f32[128,2048]{1,0:T(8,128)} fusion(f32[64,8,16,128]{3,2,1,0:T(8,128)S(1)} %bitcast.123, bf16[512,2304]{1,0:T(8,128)(2,1)S(1)} %multiply_convert_fusion.2), kind=kOutput, calls=%fused_computation.68 | convolution fusion | flops 271581184 | bytes 7471104 | tf_op jit(solution)/shard_map/dot_general | solution.py:94
  13.7 1.5 collective-permute-start.1
  17.9 2.7 %select_add_fusion.2 = f32[128,2048]{1,0:T(8,128)} fusion(f32[128,2048]{1,0:T(8,128)} %fusion.46, f32[128,2048]{1,0:T(8,128)} %collective-permute-done.1, f32[2048]{0:T(1024)S(1)} %broadcast_bitcast_fusion.2, pred[]{:T(512)} %eq.119), kind=kLoop, calls=%fused_computation.71 | loop fusion | flops 1048576 | bytes 3153921 | tf_op jit(solution)/shard_map/add | solution.py:64
  20.6 1.5 collective-permute-start.3
  25.6 19.8 %collective-permute-done.4 = f32[16]{0:T(128)S(1)} collective-permute-done((f32[16]{0:T(128)S(1)}, f32[16]{0:T(128)S(1)}, u32[]{:S(2)}, u32[]{:S(2)}) %collective-permute-start.4) | collective-permute-done | bytes 96 | tf_op jit(solution)/shard_map/ppermute | solution.py:14
  45.4 2.7 %select_add_fusion.1 = f32[128,2048]{1,0:T(8,128)} fusion(f32[128,2048]{1,0:T(8,128)} %select_add_fusion.2, f32[128,2048]{1,0:T(8,128)} %collective-permute-done.3, f32[2048]{0:T(1024)S(1)} %broadcast_bitcast_fusion.1, pred[]{:T(512)} %eq.118), kind=kLoop, calls=%fused_computation.70 | loop fusion | flops 1048576 | bytes 3153921 | tf_op jit(solution)/shard_map/add | solution.py:64
  48.1 1.7 collective-permute-start.5
  51.6 20.8 %collective-permute-done.6 = f32[16]{0:T(128)S(1)} collective-permute-done((f32[16]{0:T(128)S(1)}, f32[16]{0:T(128)S(1)}, u32[]{:S(2)}, u32[]{:S(2)}) %collective-permute-start.6) | collective-permute-done | bytes 96 | tf_op jit(solution)/shard_map/ppermute | solution.py:14
  72.7 2.7 %select_add_fusion = f32[128,2048]{1,0:T(8,128)} fusion(f32[128,2048]{1,0:T(8,128)} %select_add_fusion.1, f32[128,2048]{1,0:T(8,128)} %collective-permute-done.5, f32[2048]{0:T(1024)S(1)} %broadcast_bitcast_fusion, pred[]{:T(512)} %eq.117), kind=kLoop, calls=%fused_computation.69 | loop fusion | flops 1048576 | bytes 3153921 | tf_op jit(solution)/shard_map/add | solution.py:64
  76.9 20.9 %multiply_convert_fusion.5 = bf16[16,512,512]{2,1,0:T(8,128)(2,1)} fusion(f32[512,512]{1,0:T(8,128)S(1)} %fusion.58, f32[16,512]{1,0:T(8,128)S(1)} %copy_bitcast_fusion, f32[16,512]{1,0:T(8,128)S(1)} %get-tuple-element.297, f32[16,512]{1,0:T(8,128)S(1)} %get-tuple-element.298, f32[16,512]{1,0:T(8,128)S(1)} %get-tuple-element.299, ...), kind=kLoop, calls=%fused_computation.25.clone.clone.1 | loop fusion | flops 62914560 | bytes 12681216 | tf_op jit(solution)/shard_map/hts,shp->thp/dot_general | solution.py:44
  97.8 1.6 slice.127
  99.4 3.9 %copy.55 = bf16[512,2048]{0,1:T(8,128)(2,1)} copy(bf16[512,2048]{1,0:T(8,128)(2,1)} %slice.127) | data formatting | bytes 4194304 | tf_op jit(solution)/shard_map/slice | solution.py:83
  103.4 8.8 %fusion.13 = f32[16,128,512]{2,1,0:T(8,128)} fusion(bf16[512,16,128]{0,2,1:T(8,128)(2,1)} %bitcast.130, bf16[16,512,512]{2,1,0:T(8,128)(2,1)} %multiply_convert_fusion.5), kind=kOutput, calls=%fused_computation.26 | convolution fusion | flops 1073741824 | bytes 14680064 | tf_op jit(solution)/shard_map/hts,shp->thp/dot_general | solution.py:44
  112.2 5.4 %copy.67 = f32[512,2048]{1,0:T(8,128)} copy(f32[512,2048]{0,1:T(8,128)} %bitcast.122) | data formatting | bytes 8388608 | tf_op jit(solution)/shard_map/reshape | solution.py:45
  117.6 12.0 %conditional.4 = (f32[512,2048]{1,0:T(8,128)}) conditional(s32[]{:T(128)} %convert_element_type.517, () %tuple.29, (f32[512,128]{1,0:T(8,128)S(1)}, f32[128,2048]{1,0:T(8,128)}, f32[16,14,512]{2,0,1:T(8,128)S(1)}, pred[]{:T(512)}, f32[16,512]{1,0:T(8,128)S(1)}, /*index=5*/f32[16,512]{0,1:T(8,128)S(1)}) %tuple.85), branch_computations={%region_2.3_spmd, %region_3.4_spmd} | conditional | flops 1611677696 | bytes 15040521 | solution.py:119
  117.8 2.4 %copy.59 = f32[16,14,512]{0,2,1:T(8,128)} copy(f32[16,14,512]{2,0,1:T(8,128)S(1)} %get-tuple-element.258) | data formatting | bytes 917504 | tf_op jit(solution)/shard_map
  122.4 7.2 %bitcast_multiply_fusion = f32[512,2048]{1,0:T(8,128)} fusion(f32[64,8,16,128]{3,2,1,0:T(8,128)S(1)} %bitcast.124, f32[512,128]{1,0:T(8,128)S(1)} %get-tuple-element.74, f32[128,2048]{1,0:T(8,128)} %get-tuple-element.75), kind=kOutput, calls=%fused_computation | convolution fusion | flops 1611661312 | bytes 9699328 | tf_op jit(solution)/shard_map/cond/branch_1_fun/dot_general | solution.py:68
  129.6 12.9 %conditional.5 = (f32[512,2048]{1,0:T(8,128)}) conditional(s32[]{:T(128)} %convert_element_type.516, f32[512,2048]{1,0:T(8,128)} %get-tuple-element.322, (f32[512,128]{1,0:T(8,128)S(1)}, f32[128,2048]{1,0:T(8,128)}, f32[16,14,512]{2,0,1:T(8,128)S(1)}, f32[512,2048]{1,0:T(8,128)}, pred[]{:T(512)}, /*index=5*/f32[16,512]{1,0:T(8,128)S(1)}, ...), branch_computations={%region_4.5_spmd, %region_5.6_spmd} | conditional | flops 1612734464 | bytes 19234888 | solution.py:119
  129.6 2.4 %copy.61 = f32[16,14,512]{0,2,1:T(8,128)} copy(f32[16,14,512]{2,0,1:T(8,128)S(1)} %get-tuple-element.264) | data formatting | bytes 917504 | tf_op jit(solution)/shard_map
  134.3 8.2 %fusion.2 = f32[512,2048]{1,0:T(8,128)} fusion(f32[512,2048]{1,0:T(8,128)} %get-tuple-element.77, f32[64,8,16,128]{3,2,1,0:T(8,128)S(1)} %bitcast.126, f32[512,128]{1,0:T(8,128)S(1)} %get-tuple-element.78, f32[128,2048]{1,0:T(8,128)} %get-tuple-element.79), kind=kOutput, calls=%fused_computation.6 | convolution fusion | flops 1612709888 | bytes 13893632 | tf_op jit(solution)/shard_map/cond/branch_1_fun/dot_general | solution.py:68
  142.5 12.9 %conditional.6 = (f32[512,2048]{1,0:T(8,128)}) conditional(s32[]{:T(128)} %convert_element_type.515, f32[512,2048]{1,0:T(8,128)} %get-tuple-element.323, (f32[512,128]{1,0:T(8,128)S(1)}, f32[128,2048]{1,0:T(8,128)}, f32[16,14,512]{2,0,1:T(8,128)S(1)}, f32[512,2048]{1,0:T(8,128)}, pred[]{:T(512)}, /*index=5*/f32[16,512]{1,0:T(8,128)S(1)}, ...), branch_computations={%region_6.7_spmd, %region_7.8_spmd} | conditional | flops 1612734464 | bytes 19234888 | solution.py:119
  142.5 2.4 %copy.63 = f32[16,14,512]{0,2,1:T(8,128)} copy(f32[16,14,512]{2,0,1:T(8,128)S(1)} %get-tuple-element.272) | data formatting | bytes 917504 | tf_op jit(solution)/shard_map
  147.2 8.2 %fusion.6 = f32[512,2048]{1,0:T(8,128)} fusion(f32[512,2048]{1,0:T(8,128)} %get-tuple-element.81, f32[64,8,16,128]{3,2,1,0:T(8,128)S(1)} %bitcast.127, f32[512,128]{1,0:T(8,128)S(1)} %get-tuple-element.82, f32[128,2048]{1,0:T(8,128)} %get-tuple-element.83), kind=kOutput, calls=%fused_computation.13 | convolution fusion | flops 1612709888 | bytes 13893632 | tf_op jit(solution)/shard_map/cond/branch_1_fun/dot_general | solution.py:68
  155.5 12.9 %conditional.7 = (f32[512,2048]{1,0:T(8,128)}) conditional(s32[]{:T(128)} %convert_element_type.514, f32[512,2048]{1,0:T(8,128)} %get-tuple-element.324, (f32[512,128]{1,0:T(8,128)S(1)}, f32[128,2048]{1,0:T(8,128)}, f32[16,14,512]{2,0,1:T(8,128)S(1)}, pred[]{:T(512)}, pred[]{:T(512)}, /*index=5*/f32[16]{0:T(128)S(1)}, f32[16]{0:T(128)S(1)}, ...), branch_computations={%region_8.9_spmd, %region_9.10_spmd} | conditional | flops 1612734464 | bytes 19235082 | solution.py:119
  155.5 2.4 %copy.65 = f32[16,14,512]{0,2,1:T(8,128)} copy(f32[16,14,512]{2,0,1:T(8,128)S(1)} %get-tuple-element.280) | data formatting | bytes 917504 | tf_op jit(solution)/shard_map
  160.2 8.2 %fusion.10 = f32[512,2048]{1,0:T(8,128)} fusion(f32[512,2048]{1,0:T(8,128)} %get-tuple-element.85, f32[64,8,16,128]{3,2,1,0:T(8,128)S(1)} %bitcast.128, f32[512,128]{1,0:T(8,128)S(1)} %get-tuple-element.86, f32[128,2048]{1,0:T(8,128)} %get-tuple-element.87), kind=kOutput, calls=%fused_computation.20 | convolution fusion | flops 1612709888 | bytes 13893632 | tf_op jit(solution)/shard_map/cond/branch_1_fun/dot_general | solution.py:68
  168.4 6.7 %multiply_bitcast_fusion = (f32[64,8,16,128]{3,1,2,0:T(8,128)S(1)}, f32[512,2048]{1,0:T(8,128)}) fusion(f32[512,2048]{1,0:T(8,128)} %copy.67, f32[512,2048]{1,0:T(8,128)} %get-tuple-element.325), kind=kLoop, calls=%fused_computation.66 | loop fusion | flops 2097152 | bytes 16777216
  175.1 2.9 %copy.77 = f32[64,8,16,128]{3,2,1,0:T(8,128)} copy(f32[64,8,16,128]{3,1,2,0:T(8,128)S(1)} %get-tuple-element.292) | data formatting | bytes 8388608
  178.0 3.4 %reduce_sum.9 = f32[512,16]{1,0:T(8,128)S(1)} reduce(f32[512,16,128]{2,1,0:T(8,128)} %bitcast.129, f32[]{:T(128)} %constant.14.clone.1), dimensions={2}, to_apply=%region_10.11 | reduce | flops 1040384 | bytes 4227076 | tf_op jit(solution)/shard_map/reduce_sum | solution.py:127
  183.8 3.1 %fusion.44 = bf16[512,2048]{1,0:T(8,128)(2,1)} fusion(f32[512,2048]{1,0:T(8,128)S(1)} %copy-done.2, f32[64,8,16,128]{3,2,1,0:T(8,128)S(1)} %bitcast.125, f32[2048]{0:T(1024)S(1)} %copy-done.18), kind=kLoop, calls=%fused_computation.63 | loop fusion | flops 3145728 | bytes 10493952 | tf_op jit(solution)/shard_map/convert_element_type | solution.py:128
  (94 shorter events, 27.3 us)
Async XLA Ops:
  0.0 2.1 %copy-start = (f32[16,512]{1,0:T(8,128)S(1)}, f32[16,512]{1,0:T(8,128)}, u32[]{:S(2)}) copy-start(f32[16,512]{1,0:T(8,128)} %param.15) | copy-start | bytes 98308
  0.8 4.2 %collective-permute-start = (bf16[3,2304]{1,0:T(4,128)(2,1)S(1)}, bf16[3,2304]{1,0:T(4,128)(2,1)S(1)}, u32[]{:S(2)}, u32[]{:S(2)}) collective-permute-start(bf16[3,2304]{1,0:T(4,128)(2,1)S(1)} %slice.88), channel_id=1, source_target_pairs={{0,1},{1,2},{2,3},{3,4},{4,5},{5,6},{6,7},{7,8},{8,9},{9,10},{10,1... | collective-permute-start | bytes 41480 | tf_op jit(solution)/shard_map/ppermute | solution.py:10
  13.7 4.2 %collective-permute-start.1 = (f32[128,2048]{1,0:T(8,128)}, f32[128,2048]{1,0:T(8,128)}, u32[]{:S(2)}, u32[]{:S(2)}) collective-permute-start(f32[128,2048]{1,0:T(8,128)} %fusion.46), channel_id=1, source_target_pairs={{0,1},{1,0},{2,3},{3,2},{4,5},{5,4},{6,7},{7,6},{8,9},{9,8},{10,11... | collective-permute-start | bytes 3145736 | tf_op jit(solution)/shard_map/ppermute | solution.py:14
  15.2 2.6 %collective-permute-start.2 = (f32[16]{0:T(128)S(1)}, f32[16]{0:T(128)S(1)}, u32[]{:S(2)}, u32[]{:S(2)}) collective-permute-start(f32[16]{0:T(128)S(1)} %slice_reduce_fusion.5), channel_id=1, source_target_pairs={{0,1},{1,0},{2,3},{3,2},{4,5},{5,4},{6,7},{7,6},{8,9},{9,8},{10,11... | collective-permute-start | bytes 200 | tf_op jit(solution)/shard_map/ppermute | solution.py:14
  16.7 34.1 %copy-start.3 = (f32[16,14,512]{2,0,1:T(8,128)S(1)}, f32[16,14,512]{2,0,1:T(8,128)}, u32[]{:S(2)}) copy-start(f32[16,14,512]{2,0,1:T(8,128)} %param.16) | copy-start | bytes 1376260
  20.6 24.8 %collective-permute-start.3 = (f32[128,2048]{1,0:T(8,128)}, f32[128,2048]{1,0:T(8,128)}, u32[]{:S(2)}, u32[]{:S(2)}) collective-permute-start(f32[128,2048]{1,0:T(8,128)} %select_add_fusion.2), channel_id=1, source_target_pairs={{0,2},{1,3},{2,0},{3,1},{4,6},{5,7},{6,4},{7,5},{8,10},{9,11},{10,... | collective-permute-start | bytes 3145736 | tf_op jit(solution)/shard_map/ppermute | solution.py:14
  25.6 19.8 %collective-permute-start.4 = (f32[16]{0:T(128)S(1)}, f32[16]{0:T(128)S(1)}, u32[]{:S(2)}, u32[]{:S(2)}) collective-permute-start(f32[16]{0:T(128)S(1)} %get-tuple-element.308), channel_id=1, source_target_pairs={{0,2},{1,3},{2,0},{3,1},{4,6},{5,7},{6,4},{7,5},{8,10},{9,11},{10,... | collective-permute-start | bytes 200 | tf_op jit(solution)/shard_map/ppermute | solution.py:14
  48.1 24.6 %collective-permute-start.5 = (f32[128,2048]{1,0:T(8,128)}, f32[128,2048]{1,0:T(8,128)}, u32[]{:S(2)}, u32[]{:S(2)}) collective-permute-start(f32[128,2048]{1,0:T(8,128)} %select_add_fusion.1), channel_id=1, source_target_pairs={{0,4},{1,5},{2,6},{3,7},{4,0},{5,1},{6,2},{7,3},{8,12},{9,13},{10,... | collective-permute-start | bytes 3145736 | tf_op jit(solution)/shard_map/ppermute | solution.py:14
  51.4 20.9 %collective-permute-start.6 = (f32[16]{0:T(128)S(1)}, f32[16]{0:T(128)S(1)}, u32[]{:S(2)}, u32[]{:S(2)}) collective-permute-start(f32[16]{0:T(128)S(1)} %get-tuple-element.306), channel_id=1, source_target_pairs={{0,4},{1,5},{2,6},{3,7},{4,0},{5,1},{6,2},{7,3},{8,12},{9,13},{10,... | collective-permute-start | bytes 200 | tf_op jit(solution)/shard_map/ppermute | solution.py:14
  51.4 25.4 %copy-start.4 = (pred[512,512]{1,0:T(8,128)(4,1)S(1)}, pred[512,512]{1,0:T(8,128)(4,1)}, u32[]{:S(2)}) copy-start(pred[512,512]{1,0:T(8,128)(4,1)} %get-tuple-element.314) | copy-start | bytes 786436
  51.4 25.4 %copy-start.5 = (pred[512,512]{1,0:T(8,128)(4,1)S(1)}, pred[512,512]{1,0:T(8,128)(4,1)}, u32[]{:S(2)}) copy-start(pred[512,512]{1,0:T(8,128)(4,1)} %get-tuple-element.315) | copy-start | bytes 786436
  51.4 25.4 %copy-start.6 = (pred[512,512]{1,0:T(8,128)(4,1)S(1)}, pred[512,512]{1,0:T(8,128)(4,1)}, u32[]{:S(2)}) copy-start(pred[512,512]{1,0:T(8,128)(4,1)} %get-tuple-element.316) | copy-start | bytes 786436
  51.4 25.4 %copy-start.7 = (pred[512,512]{1,0:T(8,128)(4,1)S(1)}, pred[512,512]{1,0:T(8,128)(4,1)}, u32[]{:S(2)}) copy-start(pred[512,512]{1,0:T(8,128)(4,1)} %get-tuple-element.317) | copy-start | bytes 786436
  51.5 25.4 %copy-start.8 = (pred[512,512]{1,0:T(8,128)(4,1)S(1)}, pred[512,512]{1,0:T(8,128)(4,1)}, u32[]{:S(2)}) copy-start(pred[512,512]{1,0:T(8,128)(4,1)} %get-tuple-element.318) | copy-start | bytes 786436
  51.5 25.4 %copy-start.9 = (pred[512,512]{1,0:T(8,128)(4,1)S(1)}, pred[512,512]{1,0:T(8,128)(4,1)}, u32[]{:S(2)}) copy-start(pred[512,512]{1,0:T(8,128)(4,1)} %get-tuple-element.319) | copy-start | bytes 786436
  51.5 25.4 %copy-start.10 = (pred[512,512]{1,0:T(8,128)(4,1)S(1)}, pred[512,512]{1,0:T(8,128)(4,1)}, u32[]{:S(2)}) copy-start(pred[512,512]{1,0:T(8,128)(4,1)} %get-tuple-element.320) | copy-start | bytes 786436
  51.5 25.4 %copy-start.11 = (pred[512,512]{1,0:T(8,128)(4,1)S(1)}, pred[512,512]{1,0:T(8,128)(4,1)}, u32[]{:S(2)}) copy-start(pred[512,512]{1,0:T(8,128)(4,1)} %get-tuple-element.321) | copy-start | bytes 786436
  51.5 25.4 %copy-start.12 = (pred[512,512]{1,0:T(8,128)(4,1)S(1)}, pred[512,512]{1,0:T(8,128)(4,1)}, u32[]{:S(2)}) copy-start(pred[512,512]{1,0:T(8,128)(4,1)} %broadcast_compare_fusion.9) | copy-start | bytes 786436
  51.5 25.4 %copy-start.13 = (f32[16,512]{1,0:T(8,128)S(1)}, f32[16,512]{1,0:T(8,128)}, u32[]{:S(2)}) copy-start(f32[16,512]{1,0:T(8,128)} %get-tuple-element.301) | copy-start | bytes 98308
  51.5 25.4 %copy-start.14 = (f32[16,512]{1,0:T(8,128)S(1)}, f32[16,512]{1,0:T(8,128)}, u32[]{:S(2)}) copy-start(f32[16,512]{1,0:T(8,128)} %get-tuple-element.302) | copy-start | bytes 98308
  51.5 25.4 %copy-start.15 = (f32[16,512]{1,0:T(8,128)S(1)}, f32[16,512]{1,0:T(8,128)}, u32[]{:S(2)}) copy-start(f32[16,512]{1,0:T(8,128)} %get-tuple-element.303) | copy-start | bytes 98308
  51.5 25.4 %copy-start.16 = (f32[16,512]{1,0:T(8,128)S(1)}, f32[16,512]{1,0:T(8,128)}, u32[]{:S(2)}) copy-start(f32[16,512]{1,0:T(8,128)} %get-tuple-element.304) | copy-start | bytes 98308
  51.5 25.4 %copy-start.17 = (f32[16,512]{1,0:T(8,128)S(1)}, f32[16,512]{1,0:T(8,128)}, u32[]{:S(2)}) copy-start(f32[16,512]{1,0:T(8,128)} %get-tuple-element.305) | copy-start | bytes 98308
  75.4 80.0 %collective-permute-start.7 = (f32[128,2048]{1,0:T(8,128)}, f32[128,2048]{1,0:T(8,128)}, u32[]{:S(2)}, u32[]{:S(2)}) collective-permute-start(f32[128,2048]{1,0:T(8,128)} %select_add_fusion), channel_id=1, source_target_pairs={{0,8},{1,9},{2,10},{3,11},{4,12},{5,13},{6,14},{7,15},{8,0},{9,1},... | collective-permute-start | bytes 3145736 | tf_op jit(solution)/shard_map/ppermute | solution.py:14
  178.0 4.8 %copy-start.18 = (f32[2048]{0:T(1024)S(1)}, f32[2048]{0:T(1024)}, u32[]{:S(2)}) copy-start(f32[2048]{0:T(1024)} %param.17) | copy-start | bytes 24580
  181.6 2.2 %copy-start.2 = (f32[512,2048]{1,0:T(8,128)S(1)}, f32[512,2048]{1,0:T(8,128)}, u32[]{:S(2)}) copy-start(f32[512,2048]{1,0:T(8,128)} %get-tuple-element.293) | copy-start | bytes 12582916
  182.7 4.1 %copy-start.1 = (f32[16,512]{1,0:T(8,128)S(1)}, f32[16,512]{1,0:T(8,128)}, u32[]{:S(2)}) copy-start(f32[16,512]{1,0:T(8,128)} %param.15) | copy-start | bytes 98308
where the time goes:
time: 188 us; the launch traced here: 187 us
  other arithmetic  58.5 us (31%)
  matrix products  43.4 us (23%)
  waiting for transfers between devices  41.7 us (22%)
  local copies, waits for them, and re-layouts  35.2 us (19%)
  starting transfers between devices  7.36 us (4%)
    ppermute x7, waiting for transfers between devices, swapped(): lax.ppermute(value, axis, [(i, i ^ 1 << apart) for i in range(lax.axis_si...  41.7 us
    dot_general x4, matrix products, add_level(): jnp.dot(queries_wide, partner, precision=lax.Precision.HIGHEST, preferred...  31.9 us
    dot_general x1, other arithmetic, compute_near(): jnp.einsum('hts,shp->thp', weight, shaped, preferred_element_type=jnp.flo...  20.9 us
    another operation x9, local copies, waits for them, and re-layouts  10.1 us
    dot_general x1, matrix products, compute_near(): jnp.einsum('hts,shp->thp', weight, shaped, preferred_element_type=jnp.flo...  8.79 us
    add x3, other arithmetic, combine_groups(): return left_part * carry_decay[None, :] + right_part  8.12 us
    unnamed x1, other arithmetic  6.66 us
    ppermute x7, starting transfers between devices, swapped(): lax.ppermute(value, axis, [(i, i ^ 1 << apart) for i in range(lax.axis_si...  6.06 us
  transfers between devices with their start and end apart: 8, of which 3 were waited for; matrix products, arithmetic and copies ran while one was open for 47% of the time, Pallas kernels for 0%

commit v1 on v0

v1 whole, which is shorter than its diff:
```python
import functools
import jax
import jax.numpy as jnp
from jax import lax
from jax.experimental import pallas as pl
from jax.experimental.pallas import tpu as pltpu
from jax.sharding import PartitionSpec as P

LANES = 128
CHUNKS = 2
MESH = pl.DeviceIdType.MESH


def bits_of(number):
    return number.bit_length()


def wide(row, times):
    return jnp.concatenate([row] * times, axis=1)


def kernel(
    seq_bits, xbc, taps, decay, lw, gain, out,
    pad, halo, in_map, out_map_t, values_t, ll, ll_col, scores_t, level_code, wt, near_t,
    agg, send, node, span, span_rx, prefix,
    halo_sem, span_send, span_recv, chip_send, chip_recv, step_send, step_recv, fwd_send, fwd_recv,
):
    rows, width = xbc.shape
    heads = decay.shape[0]
    kern = taps.shape[0]
    half = heads // 2
    piece = half // CHUNKS
    tiles = rows // LANES
    tile_bits = bits_of(LANES) - 1
    local_bits = bits_of(rows) - 1
    count = 1 << seq_bits
    me = lax.axis_index("seq")
    core = lax.rem(me, 2)
    group = lax.axis_index("groups")
    after, before = lax.rem(me + 1, count), lax.rem(me + count - 1, count)

    def bit_at(k):
        return lax.rem(lax.div(me, 1 << k), 2)

    def mate(k):
        return me + (1 - 2 * bit_at(k)) * (1 << k)

    def remote(src, dst, s, r, to):
        return pltpu.make_async_remote_copy(
            src_ref=src, dst_ref=dst, send_sem=s, recv_sem=r,
            device_id=(group, to), device_id_type=MESH,
        )

    barrier = pltpu.get_barrier_semaphore()
    for to in [after, before] + [mate(k) for k in range(seq_bits)]:
        pl.semaphore_signal(barrier, inc=1, device_id=(group, to), device_id_type=MESH)

    tri = (
        lax.broadcasted_iota(jnp.int32, (rows, rows), 0)
        <= lax.broadcasted_iota(jnp.int32, (rows, rows), 1)
    ).astype(jnp.float32).astype(jnp.bfloat16)
    rest = decay[...]
    total = jnp.zeros((heads, rows), jnp.float32)
    parts = []
    for _ in range(3):
        part = rest.astype(jnp.bfloat16)
        rest = rest - part.astype(jnp.float32)
        parts.append(part)
    for part in reversed(parts):
        total = total + jnp.dot(part, tri, preferred_element_type=jnp.float32)
    for h in range(heads):
        ll[h] = total[h : h + 1]
    span[0] = jnp.broadcast_to(total[:, rows - 1 :], (heads, LANES))
    flipped = jnp.transpose(
        jnp.concatenate([total, jnp.zeros((LANES - heads, rows), jnp.float32)], axis=0)
    )
    for h in range(heads):
        ll_col[h] = jnp.broadcast_to(flipped[:, h : h + 1], (rows, LANES))
    s_pos = lax.broadcasted_iota(jnp.int32, (LANES, LANES), 0)
    t_pos = lax.broadcasted_iota(jnp.int32, (LANES, LANES), 1)
    differ = jnp.bitwise_xor(s_pos, t_pos)
    code = jnp.zeros((LANES, LANES), jnp.int32)
    for p in range(tile_bits):
        code = code + (differ >= 1 << p).astype(jnp.int32)
    level_code[...] = code

    @pl.loop(0, width // LANES)
    def _(j):
        at = pl.ds(pl.multiple_of(j * LANES, LANES), LANES)
        pad[j, 8 : 8 + rows, :] = xbc[:, at].astype(jnp.float32)

    pl.semaphore_wait(barrier, 2 + seq_bits)

    halo_copy = remote(
        xbc.at[rows - 16 : rows, :], halo, halo_sem.at[0], halo_sem.at[1], after
    )
    halo_copy.start()

    def span_copy(k):
        return remote(span.at[k], span_rx.at[k], span_send.at[k], span_recv.at[k], mate(k))

    span_copy(0).start()
    halo_copy.wait()

    @pl.loop(0, width // LANES)
    def _(j):
        at = pl.ds(pl.multiple_of(j * LANES, LANES), LANES)
        pad[j, 0:8, :] = jnp.where(me == 0, 0.0, halo[:, at].astype(jnp.float32)[8:16])

    def conv(j):
        at = pl.ds(pl.multiple_of(j * LANES, LANES), LANES)
        weights = taps[:, at]
        first = 8 - kern + 1
        total = pad[j, first : first + rows, :] * weights[0:1]
        for k in range(1, kern):
            total = total + pad[j, first + k : first + k + rows, :] * weights[k : k + 1]
        return (total / (1.0 + jnp.exp(-total))).astype(jnp.bfloat16)

    in_map[...] = conv(heads)
    out_map_t[...] = jnp.transpose(conv(heads + 1))

    def state(first):
        @pl.loop(0, piece)
        def _(i):
            h = first + i
            flipped = jnp.transpose(conv(h))
            values_t[h] = flipped
            row = ll[h]
            tail = jnp.exp(row[:, rows - 1 :] - row)
            decayed = (flipped.astype(jnp.float32) * tail).astype(jnp.bfloat16)
            st = jnp.dot(decayed, in_map[...], preferred_element_type=jnp.float32)
            agg[h] = st
            send[0, h] = st.astype(jnp.bfloat16)

    mine, theirs = core * half, (1 - core) * half

    def chip_copy(first, slot):
        at = pl.ds(first, piece)
        return remote(
            send.at[0, at], node.at[0, at], chip_send.at[slot], chip_recv.at[slot], mate(0)
        )

    def step_copy(k, q):
        at = pl.ds(mine + q * piece, piece)
        i = k * CHUNKS + q
        return remote(send.at[k, at], node.at[k, at], step_send.at[i], step_recv.at[i], mate(k))

    def fwd_copy(k, q, first):
        at = pl.ds(first + q * piece, piece)
        i = k * CHUNKS + q
        return remote(node.at[k, at], node.at[k, at], fwd_send.at[i], fwd_recv.at[i], mate(0))

    def span_step(k):
        span_copy(k).wait()
        other = span_rx[k]
        behind = prefix[k]
        prefix[k + 1] = behind + jnp.where(bit_at(k) == 1, other, 0.0)
        span[k + 1] = span[k] + other
        if k + 1 < seq_bits:
            span_copy(k + 1).start()

    def combine(k, q):
        upper = bit_at(k) == 1

        @pl.loop(0, piece)
        def _(i):
            h = mine + q * piece + i
            own_span = span[k, pl.ds(h, 1), :]
            other_span = span_rx[k, pl.ds(h, 1), :]
            keep = jnp.exp(jnp.where(upper, own_span, other_span))
            own_factor = jnp.where(upper, 1.0, keep)
            other_factor = jnp.where(upper, keep, 1.0)
            joined = agg[h] * own_factor + node[k, h].astype(jnp.float32) * other_factor
            agg[h] = joined
            send[k + 1, h] = joined.astype(jnp.bfloat16)

    prefix[0] = jnp.zeros((heads, LANES), jnp.float32)
    spans_done = 0
    for q in range(CHUNKS):
        state(theirs + q * piece)
        chip_copy(theirs + q * piece, q).start()
        if spans_done < seq_bits:
            span_step(spans_done)
            spans_done += 1
    for q in range(CHUNKS):
        state(mine + q * piece)
        chip_copy(mine + q * piece, CHUNKS + q).start()
        chip_copy(mine + q * piece, q).wait_recv()
        if seq_bits > 1:
            combine(0, q)
            step_copy(1, q).start()
        if spans_done < seq_bits:
            span_step(spans_done)
            spans_done += 1

    scored = jnp.dot(in_map[...], out_map_t[...], preferred_element_type=jnp.float32)
    s_all = lax.broadcasted_iota(jnp.int32, (rows, rows), 0)
    t_all = lax.broadcasted_iota(jnp.int32, (rows, rows), 1)
    scores_t[...] = jnp.where(s_all <= t_all, scored, 0.0)
    wt[...] = jnp.zeros_like(wt)

    def near(h):
        for a in range(tiles):
            t_at = slice(a * LANES, (a + 1) * LANES)
            row = ll[h, :, t_at]
            for b in range(a + 1):
                s_at = slice(b * LANES, (b + 1) * LANES)
                gap = row - ll_col[h, s_at, :]
                if a == b:
                    gap = jnp.minimum(gap, 0.0)
                    code = level_code[...]
                    choices = [lw[h, l : l + 1, t_at] for l in range(tile_bits + 1)]
                    bit = 0
                    while len(choices) > 1:
                        odd = jnp.bitwise_and(code, 1 << bit) != 0
                        choices = [
                            jnp.where(odd, choices[m + 1], choices[m])
                            for m in range(0, len(choices), 2)
                        ]
                        bit += 1
                    chosen = choices[0]
                else:
                    level = tile_bits + bits_of(a ^ b)
                    chosen = lw[h, level : level + 1, t_at]
                weight = chosen * jnp.exp(gap) * scores_t[s_at, t_at]
                wt[s_at, t_at] = weight.astype(jnp.bfloat16)
        for a in range(0, tiles, 2):
            deep = min(a + 2, tiles) * LANES
            t_at = slice(a * LANES, deep)
            near_t[h, :, t_at] = jnp.dot(
                values_t[h, :, 0:deep], wt[0:deep, t_at], preferred_element_type=jnp.float32
            )

    events = [(k, q) for k in range(1, seq_bits) for q in range(CHUNKS)]
    marks = [heads * i // (len(events) + 1) for i in range(len(events) + 2)]

    def event(k, q):
        if q == 0 and spans_done <= k:
            pass
        step_copy(k, q).wait_recv()
        fwd_copy(k, q, mine).start()
        if k + 1 < seq_bits:
            combine(k, q)
            step_copy(k + 1, q).start()

    for i in range(len(events) + 1):
        while i < len(events) and spans_done < seq_bits and spans_done <= events[i][0]:
            span_step(spans_done)
            spans_done += 1

        @pl.loop(marks[i], marks[i + 1])
        def _(h):
            near(h)

        if i < len(events):
            event(*events[i])

    def far(k, h):
        upper = bit_at(k) == 1
        level = local_bits + 1 + k
        exponent = ll[h] + wide(prefix[k, pl.ds(h, 1), :], tiles)
        factor = jnp.where(upper, lw[h, level : level + 1, :] * jnp.exp(exponent), 0.0)
        product = jnp.dot(node[k, h], out_map_t[...], preferred_element_type=jnp.float32)
        return product * factor

    for q in range(CHUNKS):
        chip_copy(theirs + q * piece, CHUNKS + q).wait_recv()
    for k in range(1, seq_bits):
        for q in range(CHUNKS):
            fwd_copy(k, q, theirs).wait_recv()

    @pl.loop(0, heads)
    def _(h):
        mixed = near_t[h]
        for k in range(seq_bits):
            mixed = mixed + far(k, h)
        mean = jnp.mean(mixed * mixed, axis=0, keepdims=True)
        normed = jnp.transpose(mixed * lax.rsqrt(mean + 1e-05))
        at = pl.ds(pl.multiple_of(h * LANES, LANES), LANES)
        out[:, at] = (normed * gain[pl.ds(h, 1), :]).astype(jnp.bfloat16)

    for q in range(CHUNKS):
        chip_copy(theirs + q * piece, q).wait_send()
        chip_copy(mine + q * piece, CHUNKS + q).wait_send()
    for k in range(1, seq_bits):
        for q in range(CHUNKS):
            step_copy(k, q).wait_send()
            fwd_copy(k, q, mine).wait_send()


def on_device(xbc, conv_weight, log_decay, level_weights, gain):
    rows, width = xbc.shape
    heads = log_decay.shape[0]
    inner = gain.shape[0]
    dim = inner // heads
    seq_bits = lax.axis_size("seq").bit_length() - 1
    f32, bf16 = jnp.float32, jnp.bfloat16
    dma = pltpu.SemaphoreType.DMA
    vmem = pl.BlockSpec(memory_space=pltpu.VMEM)
    square = (heads, dim, LANES)
    return pl.pallas_call(
        functools.partial(kernel, seq_bits),
        out_shape=jax.ShapeDtypeStruct((rows, inner), bf16),
        in_specs=[vmem] * 5,
        out_specs=vmem,
        scratch_shapes=[
            pltpu.VMEM((width // LANES, rows + 8, LANES), f32),
            pltpu.VMEM((16, width), bf16),
            pltpu.VMEM((rows, LANES), bf16),
            pltpu.VMEM((LANES, rows), bf16),
            pltpu.VMEM((heads, dim, rows), bf16),
            pltpu.VMEM((heads, 1, rows), f32),
            pltpu.VMEM((heads, rows, LANES), f32),
            pltpu.VMEM((rows, rows), f32),
            pltpu.VMEM((LANES, LANES), jnp.int32),
            pltpu.VMEM((rows, rows), bf16),
            pltpu.VMEM((heads, dim, rows), f32),
            pltpu.VMEM(square, f32),
            pltpu.VMEM((seq_bits,) + square, bf16),
            pltpu.VMEM((seq_bits,) + square, bf16),
            pltpu.VMEM((seq_bits + 1, heads, LANES), f32),
            pltpu.VMEM((seq_bits, heads, LANES), f32),
            pltpu.VMEM((seq_bits + 1, heads, LANES), f32),
            dma((2,)),
            dma((seq_bits,)),
            dma((seq_bits,)),
            dma((2 * CHUNKS,)),
            dma((2 * CHUNKS,)),
            dma((seq_bits * CHUNKS,)),
            dma((seq_bits * CHUNKS,)),
            dma((seq_bits * CHUNKS,)),
            dma((seq_bits * CHUNKS,)),
        ],
        compiler_params=pltpu.CompilerParams(
            collective_id=0, has_side_effects=True, vmem_limit_bytes=60 * 1024 * 1024
        ),
        name="mixer",
    )(xbc, conv_weight, log_decay, level_weights, gain.reshape(heads, dim))


def solution(mesh):
    in_specs = (
        P(("groups", "seq"), None),
        P(),
        P(None, ("groups", "seq")),
        P(None, None, ("groups", "seq")),
        P(),
    )
    out_specs = P(("groups", "seq"), None)
    return jax.shard_map(
        on_device, mesh=mesh, in_specs=in_specs, out_specs=out_specs, check_vma=False
    )
```

time: 188 us -> 51.5 us (0.27)
  the two profiles are of different devices: /device:TPU:31 before, /device:TPU:0 now
where the time goes in v1:
time: 51.5 us; the launch traced here: 51.3 us
  Pallas kernels  46 us (89%)
  local copies, waits for them, and re-layouts  5.24 us (10%)
    pallas_call x1, Pallas kernels, on_device(): pl.pallas_call(functools.partial(kernel, seq_bits), out_shape=jax.ShapeDt...  46 us
    unnamed x2, local copies, waits for them, and re-layouts  5.24 us

profile of v1, /device:TPU:0, one launch (start us, length us, event | category | flops | bytes accessed | tf_op | source)
XLA Modules:
  0.0 51.3 jit_solution(11533281203884247601)
XLA Ops:
  0.0 2.1 %copy.6.lw = f32[16,14,512]{2,1,0:T(8,128)} copy(f32[16,14,512]{2,0,1:T(8,128)} %param.8) | data formatting | bytes 917504 | tf_op args[3]
  2.1 46.0 %mixer.1 = bf16[512,2048]{1,0:T(8,128)(2,1)} custom-call(bf16[512,2304]{1,0:T(8,128)(2,1)} %xbc.1, f32[4,2304]{1,0:T(4,128)} %taps.1, f32[16,512]{1,0:T(8,128)} %decay.1, f32[16,14,512]{2,1,0:T(8,128)} %copy.6.lw, f32[16,128]{1,0:T(8,128)} %bitcast.1), custom_call_target="tpu_custom_call" | custom-call | tf_op jit(solution)/shard_map/mixer/pallas_call | solution.py:301
  48.1 3.2 %copy.8 = bf16[512,2048]{1,0:T(8,128)(2,1)} copy(bf16[512,2048]{1,0:T(8,128)(2,1)} %mixer.1) | data formatting | bytes 4194304

commit v2 on v1

--- a/solution.py
+++ b/solution.py
@@ -7,7 +7,7 @@
 from jax.sharding import PartitionSpec as P
 
 LANES = 128
-CHUNKS = 2
+CHUNKS = 4
 MESH = pl.DeviceIdType.MESH
 
 
@@ -20,8 +20,8 @@
 
 
 def kernel(
-    seq_bits, xbc, taps, decay, lw, gain, out,
-    pad, halo, in_map, out_map_t, values_t, ll, ll_col, scores_t, level_code, wt, near_t,
+    seq_bits, xbc, taps, decay, lw_in, gain, out,
+    lw, pad, halo, in_map, out_map_t, values_t, ll, ll_col, scores_t, level_code, wt, near_t,
     agg, send, node, span, span_rx, prefix,
     halo_sem, span_send, span_recv, chip_send, chip_recv, step_send, step_recv, fwd_send, fwd_recv,
 ):
@@ -38,6 +38,10 @@
     core = lax.rem(me, 2)
     group = lax.axis_index("groups")
     after, before = lax.rem(me + 1, count), lax.rem(me + count - 1, count)
+    reach = count // 4
+    quarter = lax.div(me, reach)
+    last = seq_bits - 1
+    ahead, behind = lax.rem(me + reach, count), lax.rem(me + count - reach, count)
 
     def bit_at(k):
         return lax.rem(lax.div(me, 1 << k), 2)
@@ -52,8 +56,28 @@
         )
 
     barrier = pltpu.get_barrier_semaphore()
-    for to in [after, before] + [mate(k) for k in range(seq_bits)]:
+    for to in [after, before, ahead, behind] + [mate(k) for k in range(seq_bits)]:
         pl.semaphore_signal(barrier, inc=1, device_id=(group, to), device_id_type=MESH)
+
+    @pl.loop(0, width // LANES)
+    def _(j):
+        at = pl.ds(pl.multiple_of(j * LANES, LANES), LANES)
+        pad[j, 8 : 8 + rows, :] = xbc[:, at].astype(jnp.float32)
+
+    pl.semaphore_wait(barrier, 4 + seq_bits)
+
+    halo_copy = remote(
+        xbc.at[rows - 8 : rows, :], halo, halo_sem.at[0], halo_sem.at[1], after
+    )
+
+    @pl.when(me < count - 1)
+    def _():
+        halo_copy.start()
+
+    for h in range(heads):
+        for l in range(lw_in.shape[0]):
+            lw[h, l : l + 1, :] = lw_in[l, h : h + 1, :]
+    wt[...] = jnp.zeros_like(wt)
 
     tri = (
         lax.broadcasted_iota(jnp.int32, (rows, rows), 0)
@@ -71,6 +95,10 @@
     for h in range(heads):
         ll[h] = total[h : h + 1]
     span[0] = jnp.broadcast_to(total[:, rows - 1 :], (heads, LANES))
+    def span_copy(k):
+        return remote(span.at[k], span_rx.at[k], span_send.at[k], span_recv.at[k], mate(k))
+
+    span_copy(0).start()
     flipped = jnp.transpose(
         jnp.concatenate([total, jnp.zeros((LANES - heads, rows), jnp.float32)], axis=0)
     )
@@ -84,28 +112,16 @@
         code = code + (differ >= 1 << p).astype(jnp.int32)
     level_code[...] = code
 
+
+    @pl.when(me > 0)
+    def _():
+        halo_copy.wait_recv()
+
+
     @pl.loop(0, width // LANES)
     def _(j):
         at = pl.ds(pl.multiple_of(j * LANES, LANES), LANES)
-        pad[j, 8 : 8 + rows, :] = xbc[:, at].astype(jnp.float32)
-
-    pl.semaphore_wait(barrier, 2 + seq_bits)
-
-    halo_copy = remote(
-        xbc.at[rows - 16 : rows, :], halo, halo_sem.at[0], halo_sem.at[1], after
-    )
-    halo_copy.start()
-
-    def span_copy(k):
-        return remote(span.at[k], span_rx.at[k], span_send.at[k], span_recv.at[k], mate(k))
-
-    span_copy(0).start()
-    halo_copy.wait()
-
-    @pl.loop(0, width // LANES)
-    def _(j):
-        at = pl.ds(pl.multiple_of(j * LANES, LANES), LANES)
-        pad[j, 0:8, :] = jnp.where(me == 0, 0.0, halo[:, at].astype(jnp.float32)[8:16])
+        pad[j, 0:8, :] = jnp.where(me == 0, 0.0, halo[:, at].astype(jnp.float32))
 
     def conv(j):
         at = pl.ds(pl.multiple_of(j * LANES, LANES), LANES)
@@ -145,16 +161,22 @@
         i = k * CHUNKS + q
         return remote(send.at[k, at], node.at[k, at], step_send.at[i], step_recv.at[i], mate(k))
 
+    def last_copy(q, source):
+        at = pl.ds(mine + q * piece, piece)
+        i = last * CHUNKS + q
+        return remote(
+            source.at[last, at], node.at[last, at], step_send.at[i], step_recv.at[i], ahead
+        )
+
     def fwd_copy(k, q, first):
         at = pl.ds(first + q * piece, piece)
         i = k * CHUNKS + q
         return remote(node.at[k, at], node.at[k, at], fwd_send.at[i], fwd_recv.at[i], mate(0))
 
     def span_step(k):
-        span_copy(k).wait()
+        span_copy(k).wait_recv()
         other = span_rx[k]
-        behind = prefix[k]
-        prefix[k + 1] = behind + jnp.where(bit_at(k) == 1, other, 0.0)
+        prefix[k + 1] = prefix[k] + jnp.where(bit_at(k) == 1, other, 0.0)
         span[k + 1] = span[k] + other
         if k + 1 < seq_bits:
             span_copy(k + 1).start()
@@ -175,29 +197,42 @@
             send[k + 1, h] = joined.astype(jnp.bfloat16)
 
     prefix[0] = jnp.zeros((heads, LANES), jnp.float32)
-    spans_done = 0
+
+    def ship(k, q):
+        if k < last:
+            step_copy(k, q).start()
+        else:
+            @pl.when(quarter == 1)
+            def _():
+                last_copy(q, send).start()
+
+    def join(k, q):
+        if q == 0:
+            span_step(k)
+        if k + 1 < last:
+            combine(k, q)
+        elif k + 1 == last:
+            @pl.when(quarter == 1)
+            def _():
+                combine(k, q)
+        if k + 1 <= last:
+            ship(k + 1, q)
+
     for q in range(CHUNKS):
         state(theirs + q * piece)
         chip_copy(theirs + q * piece, q).start()
-        if spans_done < seq_bits:
-            span_step(spans_done)
-            spans_done += 1
-    for q in range(CHUNKS):
+        if q > 0:
+            chip_copy(mine + (q - 1) * piece, q - 1).wait_recv()
+            join(0, q - 1)
         state(mine + q * piece)
         chip_copy(mine + q * piece, CHUNKS + q).start()
-        chip_copy(mine + q * piece, q).wait_recv()
-        if seq_bits > 1:
-            combine(0, q)
-            step_copy(1, q).start()
-        if spans_done < seq_bits:
-            span_step(spans_done)
-            spans_done += 1
+    chip_copy(mine + (CHUNKS - 1) * piece, CHUNKS - 1).wait_recv()
+    join(0, CHUNKS - 1)
 
     scored = jnp.dot(in_map[...], out_map_t[...], preferred_element_type=jnp.float32)
     s_all = lax.broadcasted_iota(jnp.int32, (rows, rows), 0)
     t_all = lax.broadcasted_iota(jnp.int32, (rows, rows), 1)
     scores_t[...] = jnp.where(s_all <= t_all, scored, 0.0)
-    wt[...] = jnp.zeros_like(wt)
 
     def near(h):
         for a in range(tiles):
@@ -231,61 +266,97 @@
                 values_t[h, :, 0:deep], wt[0:deep, t_at], preferred_element_type=jnp.float32
             )
 
-    events = [(k, q) for k in range(1, seq_bits) for q in range(CHUNKS)]
-    marks = [heads * i // (len(events) + 1) for i in range(len(events) + 2)]
-
-    def event(k, q):
-        if q == 0 and spans_done <= k:
-            pass
-        step_copy(k, q).wait_recv()
-        fwd_copy(k, q, mine).start()
-        if k + 1 < seq_bits:
-            combine(k, q)
-            step_copy(k + 1, q).start()
-
-    for i in range(len(events) + 1):
-        while i < len(events) and spans_done < seq_bits and spans_done <= events[i][0]:
-            span_step(spans_done)
-            spans_done += 1
-
+    events = sorted(
+        ((k, q) for k in range(1, last) for q in range(CHUNKS)), key=lambda e: (2 * e[0] + e[1], e)
+    )
+    marks = [heads * i // len(events) for i in range(len(events) + 1)]
+    for i, (k, q) in enumerate(events):
         @pl.loop(marks[i], marks[i + 1])
         def _(h):
             near(h)
 
-        if i < len(events):
-            event(*events[i])
+        step_copy(k, q).wait_recv()
+        join(k, q)
+        fwd_copy(k, q, mine).start()
 
     def far(k, h):
         upper = bit_at(k) == 1
         level = local_bits + 1 + k
         exponent = ll[h] + wide(prefix[k, pl.ds(h, 1), :], tiles)
         factor = jnp.where(upper, lw[h, level : level + 1, :] * jnp.exp(exponent), 0.0)
-        product = jnp.dot(node[k, h], out_map_t[...], preferred_element_type=jnp.float32)
+        source = node[k, h]
+        if k == last:
+            source = jnp.where(upper, source, jnp.zeros_like(source))
+        product = jnp.dot(source, out_map_t[...], preferred_element_type=jnp.float32)
         return product * factor
 
+    def finish(first):
+        @pl.loop(0, piece)
+        def _(i):
+            h = first + i
+            mixed = near_t[h]
+            for k in range(seq_bits):
+                mixed = mixed + far(k, h)
+            mean = jnp.mean(mixed * mixed, axis=0, keepdims=True)
+            normed = jnp.transpose(mixed * lax.rsqrt(mean + 1e-05))
+            at = pl.ds(pl.multiple_of(h * LANES, LANES), LANES)
+            out[:, at] = (normed * gain[pl.ds(h, 1), :]).astype(jnp.bfloat16)
+
+    def finish_theirs(q):
+        chip_copy(theirs + q * piece, CHUNKS + q).wait_recv()
+        for k in range(1, last):
+            fwd_copy(k, q, theirs).wait_recv()
+
+        @pl.when(quarter >= 2)
+        def _():
+            fwd_copy(last, q, theirs).wait_recv()
+
+        finish(theirs + q * piece)
+
+    span_step(last)
     for q in range(CHUNKS):
-        chip_copy(theirs + q * piece, CHUNKS + q).wait_recv()
-    for k in range(1, seq_bits):
-        for q in range(CHUNKS):
-            fwd_copy(k, q, theirs).wait_recv()
-
-    @pl.loop(0, heads)
-    def _(h):
-        mixed = near_t[h]
-        for k in range(seq_bits):
-            mixed = mixed + far(k, h)
-        mean = jnp.mean(mixed * mixed, axis=0, keepdims=True)
-        normed = jnp.transpose(mixed * lax.rsqrt(mean + 1e-05))
-        at = pl.ds(pl.multiple_of(h * LANES, LANES), LANES)
-        out[:, at] = (normed * gain[pl.ds(h, 1), :]).astype(jnp.bfloat16)
-
+        @pl.when(quarter >= 2)
+        def _():
+            last_copy(q, send).wait_recv()
+
+        @pl.when(quarter == 2)
+        def _():
+            last_copy(q, node).start()
+
+        @pl.when(quarter >= 2)
+        def _():
+            fwd_copy(last, q, mine).start()
+
+        if q > 1:
+            finish_theirs(q - 2)
+        finish(mine + q * piece)
+    for q in range(max(CHUNKS - 2, 0), CHUNKS):
+        finish_theirs(q)
+
+    @pl.when(me < count - 1)
+    def _():
+        halo_copy.wait_send()
+
+    for k in range(seq_bits):
+        span_copy(k).wait_send()
     for q in range(CHUNKS):
         chip_copy(theirs + q * piece, q).wait_send()
         chip_copy(mine + q * piece, CHUNKS + q).wait_send()
-    for k in range(1, seq_bits):
-        for q in range(CHUNKS):
+        for k in range(1, last):
             step_copy(k, q).wait_send()
             fwd_copy(k, q, mine).wait_send()
+
+        @pl.when(quarter == 1)
+        def _():
+            last_copy(q, send).wait_send()
+
+        @pl.when(quarter == 2)
+        def _():
+            last_copy(q, node).wait_send()
+
+        @pl.when(quarter >= 2)
+        def _():
+            fwd_copy(last, q, mine).wait_send()
 
 
 def on_device(xbc, conv_weight, log_decay, level_weights, gain):
@@ -304,8 +375,9 @@
         in_specs=[vmem] * 5,
         out_specs=vmem,
         scratch_shapes=[
+            pltpu.VMEM((heads, level_weights.shape[1], rows), f32),
             pltpu.VMEM((width // LANES, rows + 8, LANES), f32),
-            pltpu.VMEM((16, width), bf16),
+            pltpu.VMEM((8, width), bf16),
             pltpu.VMEM((rows, LANES), bf16),
             pltpu.VMEM((LANES, rows), bf16),
             pltpu.VMEM((heads, dim, rows), bf16),
@@ -332,10 +404,10 @@
             dma((seq_bits * CHUNKS,)),
         ],
         compiler_params=pltpu.CompilerParams(
-            collective_id=0, has_side_effects=True, vmem_limit_bytes=60 * 1024 * 1024
+            collective_id=0, has_side_effects=True, vmem_limit_bytes=36 * 1024 * 1024
         ),
         name="mixer",
-    )(xbc, conv_weight, log_decay, level_weights, gain.reshape(heads, dim))
+    )(xbc, conv_weight, log_decay, level_weights.transpose(1, 0, 2), gain.reshape(heads, dim))
 
 
 def solution(mesh):

time: 51.5 us -> 39.1 us (0.76)
  the two profiles are of different devices: /device:TPU:0 before, /device:TPU:26 now
where the time goes in v2:
time: 39.1 us; the launch traced here: 38.8 us
  Pallas kernels  32.5 us (83%)
  local copies, waits for them, and re-layouts  6.23 us (16%)
    pallas_call x1, Pallas kernels, on_device(): pl.pallas_call(functools.partial(kernel, seq_bits), out_shape=jax.ShapeDt...  32.5 us
    unnamed x11, local copies, waits for them, and re-layouts  6.23 us

profile of v2, /device:TPU:26, one launch (start us, length us, event | category | flops | bytes accessed | tf_op | source)
XLA Modules:
  0.0 38.8 jit_solution(5638685622630041759)
XLA Ops:
  0.0 0.0 copy-start
  0.0 1.7 %copy-done = bf16[512,2304]{1,0:T(8,128)(2,1)S(1)} copy-done((bf16[512,2304]{1,0:T(8,128)(2,1)S(1)}, bf16[512,2304]{1,0:T(8,128)(2,1)}, u32[]{:S(2)}) %copy-start) | copy-done | bytes 2359320
  1.7 0.0 copy-start.1
  1.7 1.0 %copy-done.1 = f32[16,14,512]{2,0,1:T(8,128)S(1)} copy-done((f32[16,14,512]{2,0,1:T(8,128)S(1)}, f32[16,14,512]{2,0,1:T(8,128)}, u32[]{:S(2)}) %copy-start.1) | copy-done | bytes 458776
  2.7 0.0 copy-start.2
  2.7 0.8 %copy-done.2 = f32[4,2304]{1,0:T(4,128)S(1)} copy-done((f32[4,2304]{1,0:T(4,128)S(1)}, f32[4,2304]{1,0:T(4,128)}, u32[]{:S(2)}) %copy-start.2) | copy-done | bytes 36888
  3.5 0.0 copy-start.3
  3.5 0.8 %copy-done.3 = f32[16,512]{1,0:T(8,128)S(1)} copy-done((f32[16,512]{1,0:T(8,128)S(1)}, f32[16,512]{1,0:T(8,128)}, u32[]{:S(2)}) %copy-start.3) | copy-done | bytes 32792
  4.2 0.0 copy-start.4
  4.2 0.7 %copy-done.4 = f32[2048]{0:T(1024)S(1)} copy-done((f32[2048]{0:T(1024)S(1)}, f32[2048]{0:T(1024)}, u32[]{:S(2)}) %copy-start.4) | copy-done | bytes 8216
  4.9 32.5 %mixer.1 = bf16[512,2048]{1,0:T(8,128)(2,1)S(1)} custom-call(bf16[512,2304]{1,0:T(8,128)(2,1)S(1)} %copy-done, f32[4,2304]{1,0:T(4,128)S(1)} %copy-done.2, f32[16,512]{1,0:T(8,128)S(1)} %copy-done.3, f32[14,16,512]{2,1,0:T(8,128)S(1)} %bitcast.2, f32[16,128]{1,0:T(8,128)S(1)} %bitcast.3), custom_call_target="tpu_custom_call" | custom-call | tf_op jit(solution)/shard_map/mixer/pallas_call | solution.py:372
  37.5 1.3 %copy.7 = bf16[512,2048]{1,0:T(8,128)(2,1)} copy(bf16[512,2048]{1,0:T(8,128)(2,1)S(1)} %mixer.1) | data formatting | bytes 4194304
Async XLA Ops:
  0.0 1.7 %copy-start = (bf16[512,2304]{1,0:T(8,128)(2,1)S(1)}, bf16[512,2304]{1,0:T(8,128)(2,1)}, u32[]{:S(2)}) copy-start(bf16[512,2304]{1,0:T(8,128)(2,1)} %xbc.1) | copy-start | bytes 7077892
  1.7 1.0 %copy-start.1 = (f32[16,14,512]{2,0,1:T(8,128)S(1)}, f32[16,14,512]{2,0,1:T(8,128)}, u32[]{:S(2)}) copy-start(f32[16,14,512]{2,0,1:T(8,128)} %param.8) | copy-start | bytes 1376260
  2.7 0.8 %copy-start.2 = (f32[4,2304]{1,0:T(4,128)S(1)}, f32[4,2304]{1,0:T(4,128)}, u32[]{:S(2)}) copy-start(f32[4,2304]{1,0:T(4,128)} %taps.1) | copy-start | bytes 110596
  3.5 0.8 %copy-start.3 = (f32[16,512]{1,0:T(8,128)S(1)}, f32[16,512]{1,0:T(8,128)}, u32[]{:S(2)}) copy-start(f32[16,512]{1,0:T(8,128)} %decay.1) | copy-start | bytes 98308
  4.2 0.7 %copy-start.4 = (f32[2048]{0:T(1024)S(1)}, f32[2048]{0:T(1024)}, u32[]{:S(2)}) copy-start(f32[2048]{0:T(1024)} %param.9) | copy-start | bytes 24580

commit v3 on v2

--- a/solution.py
+++ b/solution.py
@@ -7,7 +7,7 @@
 from jax.sharding import PartitionSpec as P
 
 LANES = 128
-CHUNKS = 4
+CHUNKS = 8
 MESH = pl.DeviceIdType.MESH
 
 
@@ -20,8 +20,8 @@
 
 
 def kernel(
-    seq_bits, xbc, taps, decay, lw_in, gain, out,
-    lw, pad, halo, in_map, out_map_t, values_t, ll, ll_col, scores_t, level_code, wt, near_t,
+    seq_bits, xbc_hbm, taps_hbm, decay_hbm, lw_hbm, gain_hbm, out,
+    xbc, taps, decay, lw_in, gain, load_sem, lw, pad, halo, in_map, out_map_t, values_t, ll, ll_col, scores_t, level_code, wt, near_t,
     agg, send, node, span, span_rx, prefix,
     halo_sem, span_send, span_recv, chip_send, chip_recv, step_send, step_recv, fwd_send, fwd_recv,
 ):
@@ -55,34 +55,23 @@
             device_id=(group, to), device_id_type=MESH,
         )
 
+    loads = [
+        pltpu.make_async_copy(src, dst, load_sem.at[i])
+        for i, (src, dst) in enumerate((
+            (decay_hbm, decay), (xbc_hbm, xbc), (lw_hbm, lw_in), (taps_hbm, taps), (gain_hbm, gain)
+        ))
+    ]
+    for load in loads:
+        load.start()
     barrier = pltpu.get_barrier_semaphore()
     for to in [after, before, ahead, behind] + [mate(k) for k in range(seq_bits)]:
         pl.semaphore_signal(barrier, inc=1, device_id=(group, to), device_id_type=MESH)
-
-    @pl.loop(0, width // LANES)
-    def _(j):
-        at = pl.ds(pl.multiple_of(j * LANES, LANES), LANES)
-        pad[j, 8 : 8 + rows, :] = xbc[:, at].astype(jnp.float32)
-
-    pl.semaphore_wait(barrier, 4 + seq_bits)
-
-    halo_copy = remote(
-        xbc.at[rows - 8 : rows, :], halo, halo_sem.at[0], halo_sem.at[1], after
-    )
-
-    @pl.when(me < count - 1)
-    def _():
-        halo_copy.start()
-
-    for h in range(heads):
-        for l in range(lw_in.shape[0]):
-            lw[h, l : l + 1, :] = lw_in[l, h : h + 1, :]
-    wt[...] = jnp.zeros_like(wt)
 
     tri = (
         lax.broadcasted_iota(jnp.int32, (rows, rows), 0)
         <= lax.broadcasted_iota(jnp.int32, (rows, rows), 1)
     ).astype(jnp.float32).astype(jnp.bfloat16)
+    loads[0].wait()
     rest = decay[...]
     total = jnp.zeros((heads, rows), jnp.float32)
     parts = []
@@ -95,10 +84,34 @@
     for h in range(heads):
         ll[h] = total[h : h + 1]
     span[0] = jnp.broadcast_to(total[:, rows - 1 :], (heads, LANES))
+    pl.semaphore_wait(barrier, 4 + seq_bits)
+
+    halo_copy = remote(
+        xbc_hbm.at[rows - 8 : rows, :], halo, halo_sem.at[0], halo_sem.at[1], after
+    )
+
+    @pl.when(me < count - 1)
+    def _():
+        halo_copy.start()
+
     def span_copy(k):
         return remote(span.at[k], span_rx.at[k], span_send.at[k], span_recv.at[k], mate(k))
 
     span_copy(0).start()
+    loads[1].wait()
+
+    @pl.loop(0, width // LANES)
+    def _(j):
+        at = pl.ds(pl.multiple_of(j * LANES, LANES), LANES)
+        pad[j, 8 : 8 + rows, :] = xbc[:, at].astype(jnp.float32)
+
+    loads[2].wait()
+    for h in range(heads):
+        for l in range(lw_in.shape[0]):
+            lw[h, l : l + 1, :] = lw_in[l, h : h + 1, :]
+    wt[...] = jnp.zeros_like(wt)
+    loads[3].wait()
+    loads[4].wait()
     flipped = jnp.transpose(
         jnp.concatenate([total, jnp.zeros((LANES - heads, rows), jnp.float32)], axis=0)
     )
@@ -267,7 +280,7 @@
             )
 
     events = sorted(
-        ((k, q) for k in range(1, last) for q in range(CHUNKS)), key=lambda e: (2 * e[0] + e[1], e)
+        ((k, q) for k in range(1, last) for q in range(CHUNKS)), key=lambda e: (3 * e[0] + e[1], e)
     )
     marks = [heads * i // len(events) for i in range(len(events) + 1)]
     for i, (k, q) in enumerate(events):
@@ -368,13 +381,20 @@
     f32, bf16 = jnp.float32, jnp.bfloat16
     dma = pltpu.SemaphoreType.DMA
     vmem = pl.BlockSpec(memory_space=pltpu.VMEM)
+    hbm = pl.BlockSpec(memory_space=pltpu.HBM)
     square = (heads, dim, LANES)
     return pl.pallas_call(
         functools.partial(kernel, seq_bits),
         out_shape=jax.ShapeDtypeStruct((rows, inner), bf16),
-        in_specs=[vmem] * 5,
+        in_specs=[hbm] * 5,
         out_specs=vmem,
         scratch_shapes=[
+            pltpu.VMEM((rows, width), bf16),
+            pltpu.VMEM(conv_weight.shape, f32),
+            pltpu.VMEM((heads, rows), f32),
+            pltpu.VMEM((level_weights.shape[1], heads, rows), f32),
+            pltpu.VMEM((heads, dim), f32),
+            dma((5,)),
             pltpu.VMEM((heads, level_weights.shape[1], rows), f32),
             pltpu.VMEM((width // LANES, rows + 8, LANES), f32),
             pltpu.VMEM((8, width), bf16),
@@ -404,7 +424,7 @@
             dma((seq_bits * CHUNKS,)),
         ],
         compiler_params=pltpu.CompilerParams(
-            collective_id=0, has_side_effects=True, vmem_limit_bytes=36 * 1024 * 1024
+            collective_id=0, has_side_effects=True, vmem_limit_bytes=60 * 1024 * 1024
         ),
         name="mixer",
     )(xbc, conv_weight, log_decay, level_weights.transpose(1, 0, 2), gain.reshape(heads, dim))

time: 39.1 us -> 37.6 us (0.962)
  the two profiles are of different devices: /device:TPU:26 before, /device:TPU:25 now
where the time goes in v3:
time: 37.6 us; the launch traced here: 37.4 us
  Pallas kernels  34.3 us (91%)
  local copies, waits for them, and re-layouts  3.16 us (8%)
    pallas_call x1, Pallas kernels, on_device(): pl.pallas_call(functools.partial(kernel, seq_bits), out_shape=jax.ShapeDt...  34.3 us
    unnamed x1, local copies, waits for them, and re-layouts  3.16 us

profile of v3, /device:TPU:25, one launch (start us, length us, event | category | flops | bytes accessed | tf_op | source)
XLA Modules:
  0.0 37.4 jit_solution(10058627467507091462)
XLA Ops:
  0.0 34.3 %mixer.1 = bf16[512,2048]{1,0:T(8,128)(2,1)} custom-call(bf16[512,2304]{1,0:T(8,128)(2,1)} %xbc_hbm.1, f32[4,2304]{1,0:T(4,128)} %taps_hbm.1, f32[16,512]{1,0:T(8,128)} %decay_hbm.1, f32[14,16,512]{2,1,0:T(8,128)} %bitcast.2, f32[16,128]{1,0:T(8,128)} %bitcast.3), custom_call_target="tpu_custom_call" | custom-call | tf_op jit(solution)/shard_map/mixer/pallas_call | solution.py:386
  34.3 3.2 %copy.7 = bf16[512,2048]{1,0:T(8,128)(2,1)} copy(bf16[512,2048]{1,0:T(8,128)(2,1)} %mixer.1) | data formatting | bytes 4194304

commit v4 on v3

--- a/solution.py
+++ b/solution.py
@@ -20,8 +20,8 @@
 
 
 def kernel(
-    seq_bits, xbc_hbm, taps_hbm, decay_hbm, lw_hbm, gain_hbm, out,
-    xbc, taps, decay, lw_in, gain, load_sem, lw, pad, halo, in_map, out_map_t, values_t, ll, ll_col, scores_t, level_code, wt, near_t,
+    seq_bits, xbc_hbm, taps_hbm, decay_hbm, lw_hbm, gain_hbm, out_hbm,
+    out, out_sem, xbc, taps, decay, lw_in, gain, load_sem, lw, pad, halo, in_map, out_map_t, values_t, ll, ll_col, scores_t, level_code, wt, near_t,
     agg, send, node, span, span_rx, prefix,
     halo_sem, span_send, span_recv, chip_send, chip_recv, step_send, step_recv, fwd_send, fwd_recv,
 ):
@@ -303,6 +303,10 @@
         product = jnp.dot(source, out_map_t[...], preferred_element_type=jnp.float32)
         return product * factor
 
+    def out_copy(h):
+        at = pl.ds(pl.multiple_of(h * LANES, LANES), LANES)
+        return pltpu.make_async_copy(out.at[:, at], out_hbm.at[:, at], out_sem.at[h])
+
     def finish(first):
         @pl.loop(0, piece)
         def _(i):
@@ -314,6 +318,7 @@
             normed = jnp.transpose(mixed * lax.rsqrt(mean + 1e-05))
             at = pl.ds(pl.multiple_of(h * LANES, LANES), LANES)
             out[:, at] = (normed * gain[pl.ds(h, 1), :]).astype(jnp.bfloat16)
+            out_copy(h).start()
 
     def finish_theirs(q):
         chip_copy(theirs + q * piece, CHUNKS + q).wait_recv()
@@ -345,6 +350,10 @@
         finish(mine + q * piece)
     for q in range(max(CHUNKS - 2, 0), CHUNKS):
         finish_theirs(q)
+
+    @pl.loop(0, heads)
+    def _(h):
+        out_copy(h).wait()
 
     @pl.when(me < count - 1)
     def _():
@@ -380,15 +389,16 @@
     seq_bits = lax.axis_size("seq").bit_length() - 1
     f32, bf16 = jnp.float32, jnp.bfloat16
     dma = pltpu.SemaphoreType.DMA
-    vmem = pl.BlockSpec(memory_space=pltpu.VMEM)
     hbm = pl.BlockSpec(memory_space=pltpu.HBM)
     square = (heads, dim, LANES)
     return pl.pallas_call(
         functools.partial(kernel, seq_bits),
         out_shape=jax.ShapeDtypeStruct((rows, inner), bf16),
         in_specs=[hbm] * 5,
-        out_specs=vmem,
+        out_specs=hbm,
         scratch_shapes=[
+            pltpu.VMEM((rows, inner), bf16),
+            dma((heads,)),
             pltpu.VMEM((rows, width), bf16),
             pltpu.VMEM(conv_weight.shape, f32),
             pltpu.VMEM((heads, rows), f32),

time: 37.6 us -> 37 us (0.984)
  Pallas kernels: 34.3 us -> 33.7 us
    pallas_call x1, Pallas kernels: 34.3 us -> 33.7 us  [on_device(): pl.pallas_call(functools.partial(kernel, seq_bits), out_shape=jax.ShapeDt...]
where the time goes in v4:
time: 37 us; the launch traced here: 36.9 us
  Pallas kernels  33.7 us (91%)
  local copies, waits for them, and re-layouts  3.16 us (9%)
    pallas_call x1, Pallas kernels, on_device(): pl.pallas_call(functools.partial(kernel, seq_bits), out_shape=jax.ShapeDt...  33.7 us
    unnamed x1, local copies, waits for them, and re-layouts  3.16 us

profile of v4, /device:TPU:25, one launch (start us, length us, event | category | flops | bytes accessed | tf_op | source)
XLA Modules:
  0.0 36.9 jit_solution(1134336007951771632)
XLA Ops:
  0.0 33.7 %mixer.1 = bf16[512,2048]{1,0:T(8,128)(2,1)} custom-call(bf16[512,2304]{1,0:T(8,128)(2,1)} %xbc_hbm.1, f32[4,2304]{1,0:T(4,128)} %taps_hbm.1, f32[16,512]{1,0:T(8,128)} %decay_hbm.1, f32[14,16,512]{2,1,0:T(8,128)} %bitcast.2, f32[16,128]{1,0:T(8,128)} %bitcast.3), custom_call_target="tpu_custom_call" | custom-call | tf_op jit(solution)/shard_map/mixer/pallas_call | solution.py:394
  33.7 3.2 %copy.7 = bf16[512,2048]{1,0:T(8,128)(2,1)} copy(bf16[512,2048]{1,0:T(8,128)(2,1)} %mixer.1) | data formatting | bytes 4194304
